TPU v7x, 1024 devices: a whole 8x8x8 slice. The times are simulated.
1024 devices in a mesh: pipe: 8 (over y_lo, core), ctx: 16 (over z, y_hi), tp: 8 (over x).
Axes of the slice: x: 8, y: 8 (y_hi: 2, y_lo: 4; y = y_hi * 4 + y_lo), z: 8, core: 2. Of those that a mesh axis runs over, the one named last changes fastest.
Arguments:
- queries: bfloat16 [8, 2048, 4096], P('pipe', 'ctx', 'tp'), may hold values from -15 to 15
- keys: bfloat16 [8, 2048, 1024], P('pipe', 'ctx', 'tp'), may hold values from -5 to 5
- values: bfloat16 [8, 2048, 1024], P('pipe', 'ctx', 'tp'), may hold values from -5 to 5
- span_ids: int32 [8, 32], P('pipe', 'ctx'), may hold values from 0 to 31, each once within a row
- cotangent: bfloat16 [8, 2048, 4096], P('pipe', 'ctx'), may hold values from -6 to 6
Outputs:
- attention: bfloat16 [8, 2048, 4096], P('pipe', 'ctx', 'tp')
- grad_out: bfloat16 [8, 4096, 4096], P('pipe', 'ctx', 'tp')
Inputs may be any that keep to these rules, and one draw needn't show every extreme that they name: `span_ids`: each row is a permutation of 0 to 31.
All inputs are finite; a program needn't handle non-finite values.
Results may differ from a plain program's by a relative error of at most 0.015.
Values may be sent and summed in bfloat16 or wider, within the bound.
A program may use at most 32 MiB of HBM per device.

v0:
```python
import math

import jax
import jax.numpy as jnp
from jax import lax
from jax.sharding import PartitionSpec as P

HQ = 32
HK = 8
HD = 128


def from_partner(x, axis, apart):
    return lax.ppermute(x, axis, [(i, i ^ 1 << apart) for i in range(lax.axis_size(axis))])


def local(queries, keys, values, span_ids, cotangent):
    tokens = queries.shape[1]
    span = tokens // 2
    group = HQ // HK
    kv_heads = keys.shape[2] // HD
    scale = 1.0 / math.sqrt(HD)
    table = lax.all_gather(span_ids, "ctx", axis=1, tiled=True)[0]
    rows = jnp.arange(tokens, dtype=jnp.int32)
    query_pos = jnp.take(span_ids[0], rows // span) * span + rows % span
    query_heads = queries[0].reshape(tokens, kv_heads, group, HD).transpose(1, 2, 0, 3)
    start_top = jnp.full((kv_heads, group, tokens), -1e30, jnp.float32)
    top = start_top
    key_piece = lax.all_gather(keys, "ctx", axis=1, tiled=True)
    value_piece = lax.all_gather(values, "ctx", axis=1, tiled=True)
    count = key_piece.shape[1]
    key_block = key_piece[0].reshape(count, kv_heads, HD)
    value_block = value_piece[0].reshape(count, kv_heads, HD)
    scores = (
        jnp.einsum("kgtd,nkd->kgtn", query_heads, key_block, preferred_element_type=jnp.float32)
        * scale
    )
    key_rows = jnp.arange(count, dtype=jnp.int32)
    key_pos = jnp.take(table, key_rows // span) * span + key_rows % span
    visible = key_pos[None, :] <= query_pos[:, None]
    masked = jnp.where(visible, scores, -1e30)
    new_top = jnp.maximum(top, jnp.max(masked, axis=-1))
    weights = jnp.where(visible, jnp.exp(scores - new_top[..., None]), 0.0)
    total = jnp.sum(weights, axis=-1)
    mixed = jnp.einsum(
        "kgtn,nkd->kgtd",
        weights.astype(jnp.bfloat16),
        value_block,
        preferred_element_type=jnp.float32,
    )
    summed = mixed
    top, total, summed = (new_top, total, summed)
    output = (
        (summed / total[..., None]).transpose(2, 0, 1, 3).reshape(tokens, kv_heads * group * HD)
    )
    attention = output.astype(jnp.bfloat16)
    cot_rows = cotangent[0]
    grad_share = lax.psum_scatter(
        lax.dot_general(
            cot_rows, attention, (((0,), (0,)), ((), ())), preferred_element_type=jnp.float32
        ).astype(jnp.bfloat16),
        "ctx",
        scatter_dimension=0,
        tiled=True,
    ).astype(jnp.float32)
    top_bit = lax.axis_size("pipe").bit_length() - 2
    partner = from_partner(grad_share.astype(jnp.bfloat16), "pipe", top_bit).astype(
        grad_share.dtype
    )
    grad_out = (grad_share + partner).astype(jnp.bfloat16)
    return (attention[None], grad_out[None])


def solution(mesh):
    placed = (
        P("pipe", "ctx", "tp"),
        P("pipe", "ctx", "tp"),
        P("pipe", "ctx", "tp"),
        P("pipe", "ctx"),
        P("pipe", "ctx", None),
    )
    return jax.shard_map(
        local,
        mesh=mesh,
        in_specs=placed,
        out_specs=(P("pipe", "ctx", "tp"), P("pipe", "ctx", "tp")),
        check_vma=False,
    )
```

profile of v0, /device:TPU:2, one launch (start us, length us, event | category | flops | bytes accessed | tf_op | source)
XLA Modules:
  0.0 457.9 jit_solution(5113596258985890083)
XLA Ops:
  7.2 0.0 copy-start
  7.2 0.0 copy-start.2
  7.2 0.0 reduce-scatter.2.cloned.1.call-start
  7.2 1.3 dynamic-slice
  9.3 0.8 bitcast_dynamic-update-slice_fusion
  10.0 32.5 %all-reduce = s32[32]{0:T(128)S(1)} all-reduce(s32[32]{0:T(128)S(1)} %bitcast_dynamic-update-slice_fusion), channel_id=1, replica_groups=mesh['pipe'=8,'ctx'=16,'tp'=8] {'ctx'}, use_global_device_ids=true, to_apply=%add | all-reduce | flops 32 | bytes 256
  42.5 0.7 fusion.37
  43.3 0.7 fusion.38
  44.0 0.1 compare_reduce_fusion
  45.2 1.3 fusion.36
  46.5 58.7 %all_gather.10 = bf16[1,2048,128]{2,1,0:T(8,128)(2,1)S(1)} all-gather(bf16[1,128,128]{2,1,0:T(8,128)(2,1)} %param.6), channel_id=1, replica_groups=mesh['pipe'=8,'ctx'=16,'tp'=8] {'ctx'}, dimensions={1}, use_global_device_ids=true | all-gather | bytes 557056 | tf_op jit(solution)/shard_map/all_gather | solution.py:29
  105.2 0.9 reshape_squeeze.2
  106.2 1.3 fusion.31
  107.4 4.4 compare_select_fusion.1
  111.8 15.7 %fusion.25 = s32[2048]{0:T(1024)S(1)} fusion(pred[2048]{0:T(1024)(128)(4,1)S(1)} %compare_reduce_fusion, pred[2048]{0:T(1024)(128)(4,1)S(1)} %compare_reduce_fusion.1, pred[2048]{0:T(1024)(128)(4,1)S(1)} %compare_reduce_fusion.2, pred[2048]{0:T(1024)(128)(4,1)S(1)} %compare_reduce_fusion.3, pred[2048]{0:T(1024)(128)(4,1)S(1)} %compare_reduce_fusion.4, ...), kind=kLoop, calls=%fused_computation.66 | loop fusion | flops 94208 | bytes 67684 | tf_op jit(solution)/shard_map/add | solution.py:39
  127.5 0.2 broadcast_compare_fusion
  127.8 2.9 select_reduce_fusion
  130.6 0.0 copy-done.2
  130.7 0.1 copy.12
  130.8 49.6 %all_gather.11 = bf16[1,2048,128]{1,2,0:T(8,128)(2,1)S(1)} all-gather(bf16[1,128,128]{1,2,0:T(8,128)(2,1)S(1)} %copy.12), channel_id=1, replica_groups=mesh['pipe'=8,'ctx'=16,'tp'=8] {'ctx'}, dimensions={1}, use_global_device_ids=true | all-gather | bytes 557056 | tf_op jit(solution)/shard_map/all_gather | solution.py:30
  180.4 3.3 fusion.1
  183.7 0.0 copy-done.1
  183.7 1.1 fusion.9
  184.8 0.0 copy-done
  184.8 3.2 fusion
  188.0 0.0 reduce-scatter.2.cloned.1.call-update
  188.0 249.0 %reduce-scatter.2.cloned.1.call-done = bf16[256,512]{0,1:T(8,128)(2,1)} async-done(((bf16[4096,512]{0,1:T(8,128)(2,1)}), bf16[256,512]{0,1:T(8,128)(2,1)}) %reduce-scatter.2.cloned.1.call-update) | async-done | bytes 262160 | tf_op jit(solution)/shard_map/reduce_scatter | solution.py:58
  437.0 2.6 collective-permute-start
  439.6 0.8 copy.13
  440.4 8.8 %collective-permute-done = bf16[256,512]{0,1:T(8,128)(2,1)S(1)} collective-permute-done((bf16[256,512]{0,1:T(8,128)(2,1)}, bf16[256,512]{0,1:T(8,128)(2,1)S(1)}, u32[]{:S(2)}, u32[]{:S(2)}) %collective-permute-start) | collective-permute-done | bytes 262176 | tf_op jit(solution)/shard_map/ppermute | solution.py:14
  449.2 1.0 fusion.16
  450.2 0.8 copy.14
  (27 shorter events, 1.1 us)
Async XLA Ops:
  7.2 177.6 %copy-start = (bf16[1,128,4096]{2,1,0:T(8,128)(2,1)S(1)}, bf16[1,128,4096]{2,1,0:T(8,128)(2,1)}, u32[]{:S(2)}) copy-start(bf16[1,128,4096]{2,1,0:T(8,128)(2,1)} %param.9) | copy-start | bytes 3145732
  7.2 123.5 %copy-start.2 = (bf16[1,128,128]{2,1,0:T(8,128)(2,1)S(1)}, bf16[1,128,128]{2,1,0:T(8,128)(2,1)}, u32[]{:S(2)}) copy-start(bf16[1,128,128]{2,1,0:T(8,128)(2,1)} %param.7) | copy-start | bytes 98308
  7.2 429.8 %reduce-scatter.2.cloned.1.call-start = ((), (), s32[]{:S(2)}) async-start(), calls=%async_computation.1 | async-start | bytes 4456448 | tf_op jit(solution)/shard_map/reduce_scatter | solution.py:58
  130.8 52.9 %copy-start.1 = (f32[4,128,2048]{2,1,0:T(8,128)S(1)}, f32[4,128,2048]{2,1,0:T(8,128)}, u32[]{:S(2)}) copy-start(f32[4,128,2048]{2,1,0:T(8,128)} %get-tuple-element.41) | copy-start | bytes 12582916
  437.0 12.2 %collective-permute-start = (bf16[256,512]{0,1:T(8,128)(2,1)}, bf16[256,512]{0,1:T(8,128)(2,1)S(1)}, u32[]{:S(2)}, u32[]{:S(2)}) collective-permute-start(bf16[256,512]{0,1:T(8,128)(2,1)} %reduce-scatter.2.cloned.1.call-done), channel_id=1, source_target_pairs={{0,512},{128,640},{256,768},{384,896},{512,0},{640,128},{768,256},... | collective-permute-start | bytes 786440 | tf_op jit(solution)/shard_map/ppermute | solution.py:14
Sparse Core Ops, SparseCore 0:
  188.1 248.8 reduce-scatter.1
where the time goes:
time: 458 us
  waiting for transfers between devices  258 us (56%)
  blocking collectives  141 us (31%)
  other arithmetic  27.1 us (6%)
  between operations  14.8 us (3%)
  local copies, waits for them, and re-layouts  7.55 us (2%)
  matrix products  7.13 us (2%)
    reduce_scatter x1, waiting for transfers between devices, local(): lax.psum_scatter(lax.dot_general(cot_rows, attention, (((0,), (0,)), ((),...  249 us
    all_gather x1, blocking collectives, local(): key_piece = lax.all_gather(keys, 'ctx', axis=1, tiled=True)  58.7 us
    all_gather x1, blocking collectives, local(): value_piece = lax.all_gather(values, 'ctx', axis=1, tiled=True)  49.6 us
    unnamed x1, blocking collectives  32.5 us
    add x1, other arithmetic, local(): key_pos = jnp.take(table, key_rows // span) * span + key_rows % span  15.7 us
  transfers between devices with their start and end apart: 2, of which 2 were waited for; matrix products, arithmetic and copies ran while one was open for 0% of the time, Pallas kernels for 0%

commit v1 on v0

v1 whole, which is shorter than its diff:
```python
import functools
import math

import jax
import jax.numpy as jnp
from jax import lax
from jax.experimental import pallas as pl
from jax.experimental.pallas import tpu as pltpu
from jax.sharding import PartitionSpec as P

HD = 128
PAD = 16
MESH = pl.DeviceIdType.MESH
BF = jnp.bfloat16
F32 = jnp.float32


class Ring:
    def __init__(self, n, long_right, ref_of, send, recv, right, left, first=None):
        self.n = n
        self.reach = n // 2 if long_right else (n - 1) // 2
        self.ref_of, self.send, self.recv = ref_of, send, recv
        self.right, self.left, self.first = right, left, first

    def copy(self, j):
        rightward = j <= self.reach
        source = j - 1 if rightward else (j + 1) % self.n
        src = self.ref_of(source, 0)
        if source == 0 and self.first is not None:
            src = self.first
        dst = self.ref_of(j, 1 if rightward else -1)
        return pltpu.make_async_remote_copy(
            src_ref=src,
            dst_ref=dst,
            send_sem=self.send(j),
            recv_sem=self.recv(j),
            device_id=self.right if rightward else self.left,
            device_id_type=MESH,
        )

    def landed(self, j):
        dst = self.ref_of(j, 0)
        rightward = j <= self.reach
        return pltpu.make_async_remote_copy(
            src_ref=dst,
            dst_ref=dst,
            send_sem=self.send(j),
            recv_sem=self.recv(j),
            device_id=self.right if rightward else self.left,
            device_id_type=MESH,
        )

    def begin(self):
        for j in sorted({1, self.n - 1}):
            self.copy(j).start()

    def step(self, s):
        slots = []
        if s <= self.reach:
            slots.append(s)
        if s <= self.n - 1 - self.reach:
            slots.append(self.n - s)
        for j in slots:
            self.landed(j).wait_recv()
            onward = j + 1 if j <= self.reach else j - 1
            if j <= self.reach and onward <= self.reach:
                self.copy(onward).start()
            elif j > self.reach and onward > self.reach:
                self.copy(onward).start()
        return slots

    def drain(self):
        for j in range(1, self.n):
            self.copy(j).wait_send()


def kernel(
    sizes, span, q, k, v, cot, att, grad,
    kbuf, vbuf, q4, scores, tops, probs, cbuf, cot_t, abuf, acc, out1, in1, out2, in2,
    kv_send, kv_recv, y_send, y_recv, a2a_send, a2a_recv, own_sem, x_send, x_recv, att_send, att_recv,
):
    n_pipe, nz, nx = sizes
    p, c, t = lax.axis_index("pipe"), lax.axis_index("ctx"), lax.axis_index("tp")
    side = lax.rem(c, 2)
    z = lax.div(c, 2)
    tokens = q.shape[0]
    heads = q.shape[1] // HD
    span_len = tokens // 2
    feats = cot.shape[1] // nz
    chunk = tokens // nx
    half = feats // 2

    def at_z(d):
        return {"ctx": lax.rem(z + d, nz) * 2 + side}

    def at_x(d):
        return {"tp": lax.rem(t + d, nx)}

    across = c + 1 - 2 * side
    mirror = lax.rem(p + n_pipe // 2, n_pipe)
    y_peer = {"ctx": across}
    fold_peer = {"pipe": mirror, "ctx": across}
    pair_peer = {"pipe": mirror}

    barrier = pltpu.get_barrier_semaphore()
    peers = [at_z(d) for d in range(1, nz)] + [y_peer, fold_peer, pair_peer, at_x(1), at_x(nx - 1)]
    for peer in peers:
        pl.semaphore_signal(barrier, inc=1, device_id=peer, device_id_type=MESH)

    lane = lax.broadcasted_iota(jnp.int32, (PAD, HD), 1)
    id0, id1 = span[0, 0].astype(F32), span[0, 1].astype(F32)
    kbuf[0, :tokens, :] = k[...]
    kbuf[0, tokens:, :] = jnp.where(lane < span_len, id0, id1).astype(BF)
    vbuf[0, :, :] = v[...]
    for h in range(heads):
        q4[h * tokens:(h + 1) * tokens, :] = q[:, h * HD:(h + 1) * HD]
    row = lax.broadcasted_iota(jnp.int32, (tokens, HD), 0)
    col = lax.broadcasted_iota(jnp.int32, (tokens, HD), 1)
    query_pos = jnp.where(row < span_len, id0, id1) * span_len + lax.rem(row, span_len).astype(F32)
    key_off = lax.rem(col, span_len).astype(F32)

    pl.semaphore_wait(barrier, len(peers))

    def z_ring(buf, base, g, long_right, first=None):
        return Ring(
            nz, long_right, lambda j, way: buf.at[base + j],
            lambda j: kv_send.at[g, j], lambda j: kv_recv.at[g, j], at_z(1), at_z(nz - 1), first,
        )

    k_own = z_ring(kbuf, 0, 0, True)
    v_own = z_ring(vbuf, 0, 1, False, v)
    k_far = z_ring(kbuf, nz, 2, False)
    v_far = z_ring(vbuf, nz, 3, True)
    k_over = pltpu.make_async_remote_copy(
        kbuf.at[0], kbuf.at[nz], y_send.at[0], y_recv.at[0], device_id=y_peer, device_id_type=MESH)
    v_over = pltpu.make_async_remote_copy(
        v, vbuf.at[nz], y_send.at[1], y_recv.at[1], device_id=y_peer, device_id_type=MESH)
    k_over.start()
    v_over.start()
    k_own.begin()
    v_own.begin()

    rows = pl.ds(pl.multiple_of(t * chunk, chunk), chunk)

    def to_z(d):
        columns = pl.ds(pl.multiple_of(lax.rem(z + d, nz) * feats, feats), feats)
        return cot.at[rows, columns]

    own_cot = pltpu.make_async_copy(to_z(0), cbuf.at[t, 0], own_sem)
    own_cot.start()
    a2a = {
        d: pltpu.make_async_remote_copy(
            to_z(d), cbuf.at[t, d], a2a_send.at[d], a2a_recv.at[d], device_id=at_z(d), device_id_type=MESH)
        for d in range(1, nz)
    }
    for d in sorted(a2a, key=lambda d: -min(d, nz - d)):
        a2a[d].start()

    factor = math.log2(math.e) / math.sqrt(HD)

    def score(slot):
        keys = kbuf[slot, :tokens, :]
        ids = kbuf[slot, tokens:, :].astype(F32)
        key_pos = jnp.broadcast_to(ids[0:1, :], (tokens, HD)) * span_len + key_off
        bias = jnp.where(key_pos <= query_pos, 0.0, -1e30)
        for h in range(heads):
            part = lax.dot_general(
                q4[h * tokens:(h + 1) * tokens, :], keys, (((1,), (1,)), ((), ())), preferred_element_type=F32)
            part = part * factor + bias
            scores[h, slot] = part
            tops[h] = part if slot == 0 else jnp.maximum(tops[h], part)

    score(0)
    steps = nz // 2
    x_steps = nx // 2
    for s in range(1, steps + 1):
        fresh = k_own.step(s)
        v_own.step(s)
        for slot in fresh:
            score(slot)
        if s == min(2, steps):
            k_over.wait_recv()
            k_far.begin()
            v_over.wait_recv()
            v_far.begin()
            score(nz)

    low, high = (0, nz // 2), (nz // 2, nz)

    def x_ring(g, part, long_right):
        def ref_of(j, way):
            place = lax.rem(t + way - j + 2 * nx, nx)
            return cbuf.at[place, part[0]:part[1]]

        return Ring(
            nx, long_right, ref_of, lambda j: x_send.at[g, j], lambda j: x_recv.at[g, j], at_x(1), at_x(nx - 1))

    x_low, x_high = x_ring(0, low, True), x_ring(1, high, False)
    own_cot.wait()
    for d in range(1, nz // 2):
        a2a[d].wait_recv()
    x_low.begin()
    for d in range(nz // 2, nz):
        a2a[d].wait_recv()
    x_high.begin()

    def x_step(s):
        if s <= x_steps:
            x_low.step(s)
            x_high.step(s)

    for s in range(1, steps + 1):
        fresh = k_far.step(s)
        v_far.step(s)
        for slot in fresh:
            score(nz + slot)
        if s == max(steps - 1, 1):
            x_step(1)

    a_rings = [
        Ring(
            nz, h % 2 == 0, functools.partial(lambda h, j, way: abuf.at[h, j], h),
            functools.partial(lambda h, j: att_send.at[h, j], h),
            functools.partial(lambda h, j: att_recv.at[h, j], h), at_z(1), at_z(nz - 1))
        for h in range(heads)
    ]

    def attend(h):
        top = jnp.broadcast_to(jnp.max(tops[h], axis=-1, keepdims=True), (tokens, HD))
        total = jnp.zeros((tokens, HD), F32)
        for slot in range(2 * nz):
            weights = jnp.exp2(scores[h, slot] - top)
            total = total + weights
            probs[:, slot * HD:(slot + 1) * HD] = weights.astype(BF)
        mixed = jnp.dot(probs[...], vbuf[...].reshape(2 * nz * tokens, HD), preferred_element_type=F32)
        out = (mixed / jnp.sum(total, axis=-1, keepdims=True)).astype(BF)
        abuf[h, 0] = out
        att[:, h * HD:(h + 1) * HD] = out

    for h in range(heads):
        attend(h)
        a_rings[h].begin()
        if h == 0:
            x_step(2)
        if h == heads - 1:
            x_step(3)

    def turn(j):
        block = cbuf[:, j].reshape(tokens, feats)
        cot_t[:, j * tokens:(j + 1) * tokens] = block.T

    for s in range(1, steps):
        for h in range(heads):
            a_rings[h].step(s)
        if s == 1:
            x_step(4)
        if s == min(2, steps - 1):
            for j in range(nz):
                turn(j)
    if steps == 1:
        x_step(4)
        for j in range(nz):
            turn(j)

    fold = [
        pltpu.make_async_remote_copy(
            out1.at[h, 1 - side], in1.at[h], y_send.at[2 + h], y_recv.at[2 + h],
            device_id=fold_peer, device_id_type=MESH)
        for h in range(heads)
    ]
    pair = [
        pltpu.make_async_remote_copy(
            out2.at[h], in2.at[h], y_send.at[2 + heads + h], y_recv.at[2 + heads + h],
            device_id=pair_peer, device_id_type=MESH)
        for h in range(heads)
    ]
    for h in range(heads):
        a_rings[h].step(steps)
        summed = jnp.dot(cot_t[...], abuf[h].reshape(nz * tokens, HD), preferred_element_type=F32)
        acc[h] = summed.reshape(2, half, HD)
        out1[h] = summed.astype(BF).reshape(2, half, HD)
        fold[h].start()
    for h in range(heads):
        fold[h].wait_recv()
        both = acc[h, side] + in1[h].astype(F32)
        acc[h, side] = both
        out2[h] = both.astype(BF)
        pair[h].start()
    for h in range(heads):
        pair[h].wait_recv()
        grad[:, h * HD:(h + 1) * HD] = (acc[h, side] + in2[h].astype(F32)).astype(BF)

    for ring in [k_own, v_own, k_far, v_far, x_low, x_high] + a_rings:
        ring.drain()
    for copy in [k_over, v_over] + list(a2a.values()) + fold + pair:
        copy.wait_send()


def solution(mesh):
    n_pipe, n_ctx, nx = mesh.shape["pipe"], mesh.shape["ctx"], mesh.shape["tp"]
    nz = n_ctx // 2

    def local(queries, keys, values, span_ids, cotangent):
        tokens, width = queries.shape[1:]
        heads = width // HD
        feats = cotangent.shape[2] // nz
        half = feats // 2
        dma = pltpu.SemaphoreType.DMA
        vmem = pl.BlockSpec(memory_space=pltpu.VMEM)
        attention, grad = pl.pallas_call(
            functools.partial(kernel, (n_pipe, nz, nx)),
            out_shape=(
                jax.ShapeDtypeStruct((tokens, width), BF),
                jax.ShapeDtypeStruct((half, width), BF),
            ),
            in_specs=[
                pl.BlockSpec(memory_space=pltpu.SMEM), vmem, vmem, vmem, pl.BlockSpec(memory_space=pl.ANY),
            ],
            out_specs=(vmem, vmem),
            scratch_shapes=[
                pltpu.VMEM((2 * nz, tokens + PAD, HD), BF),
                pltpu.VMEM((2 * nz, tokens, HD), BF),
                pltpu.VMEM((heads * tokens, HD), BF),
                pltpu.VMEM((heads, 2 * nz, tokens, HD), F32),
                pltpu.VMEM((heads, tokens, HD), F32),
                pltpu.VMEM((tokens, 2 * nz * HD), BF),
                pltpu.VMEM((nx, nz, tokens // nx, feats), BF),
                pltpu.VMEM((feats, nz * tokens), BF),
                pltpu.VMEM((heads, nz, tokens, HD), BF),
                pltpu.VMEM((heads, 2, half, HD), F32),
                pltpu.VMEM((heads, 2, half, HD), BF),
                pltpu.VMEM((heads, half, HD), BF),
                pltpu.VMEM((heads, half, HD), BF),
                pltpu.VMEM((heads, half, HD), BF),
                dma((4, nz)),
                dma((4, nz)),
                dma((2 + 2 * heads,)),
                dma((2 + 2 * heads,)),
                dma((nz,)),
                dma((nz,)),
                dma,
                dma((2, nx)),
                dma((2, nx)),
                dma((heads, nz)),
                dma((heads, nz)),
            ],
            compiler_params=pltpu.CompilerParams(
                collective_id=0, has_side_effects=True, vmem_limit_bytes=40 * 1024 * 1024
            ),
            name="fused",
        )(span_ids, queries[0], keys[0], values[0], cotangent[0])
        return attention[None], grad[None]

    return jax.shard_map(
        local,
        mesh=mesh,
        in_specs=(
            P("pipe", "ctx", "tp"),
            P("pipe", "ctx", "tp"),
            P("pipe", "ctx", "tp"),
            P("pipe", "ctx"),
            P("pipe", "ctx", None),
        ),
        out_specs=(P("pipe", "ctx", "tp"), P("pipe", "ctx", "tp")),
        check_vma=False,
    )
```

time: 458 us -> 86.5 us (0.19)
  the two profiles are of different devices: /device:TPU:2 before, /device:TPU:4 now
where the time goes in v1:
time: 86.5 us; the launch traced here: 86 us
  Pallas kernels  79.7 us (92%)
  local copies, waits for them, and re-layouts  5.65 us (7%)
    pallas_call x1, Pallas kernels, local(): pl.pallas_call(functools.partial(kernel, (n_pipe, nz, nx)), out_shape=(ja...  79.7 us
    unnamed x12, local copies, waits for them, and re-layouts  5.65 us

profile of v1, /device:TPU:4, one launch (start us, length us, event | category | flops | bytes accessed | tf_op | source)
XLA Modules:
  0.0 86.0 jit_solution(128111918181728193)
XLA Ops:
  0.6 0.0 copy-start.4
  0.6 0.6 copy-done.4
  1.3 0.0 copy-start
  1.3 1.2 %copy-done = bf16[1,128,4096]{2,1,0:T(8,128)(2,1)S(1)} copy-done((bf16[1,128,4096]{2,1,0:T(8,128)(2,1)S(1)}, bf16[1,128,4096]{2,1,0:T(8,128)(2,1)}, u32[]{:S(2)}) %copy-start) | copy-done | bytes 1048600
  2.5 0.0 copy-start.1
  2.5 0.9 %copy-done.1 = bf16[1,128,512]{2,1,0:T(8,128)(2,1)S(1)} copy-done((bf16[1,128,512]{2,1,0:T(8,128)(2,1)S(1)}, bf16[1,128,512]{2,1,0:T(8,128)(2,1)}, u32[]{:S(2)}) %copy-start.1) | copy-done | bytes 131096
  3.4 0.0 copy-start.2
  3.4 0.8 copy-done.2
  4.2 0.0 copy-start.3
  4.2 0.8 copy-done.3
  4.9 79.7 %fused.1 = (bf16[128,512]{1,0:T(8,128)(2,1)S(1)}, bf16[256,512]{1,0:T(8,128)(2,1)S(1)}) custom-call(s32[1,2]{1,0:T(1,128)S(1)} %copy-done.4, bf16[128,512]{1,0:T(8,128)(2,1)S(1)} %bitcast.8, bf16[128,128]{1,0:T(8,128)(2,1)S(1)} %bitcast.10, bf16[128,128]{1,0:T(8,128)(2,1)S(1)} %bitcast.11, bf16[128,4096]{1,0:T(8,128)(2,1)S(1)} %bitcast.6), custom_call_target="tpu_custom_call" | custom-call | tf_op jit(solution)/shard_map/fused/pallas_call | solution.py:310
  84.7 0.7 copy.9
  85.3 0.7 copy.10
Async XLA Ops:
  0.6 0.7 copy-start.4
  1.3 1.2 %copy-start = (bf16[1,128,4096]{2,1,0:T(8,128)(2,1)S(1)}, bf16[1,128,4096]{2,1,0:T(8,128)(2,1)}, u32[]{:S(2)}) copy-start(bf16[1,128,4096]{2,1,0:T(8,128)(2,1)} %param.9) | copy-start | bytes 3145732
  2.5 0.9 %copy-start.1 = (bf16[1,128,512]{2,1,0:T(8,128)(2,1)S(1)}, bf16[1,128,512]{2,1,0:T(8,128)(2,1)}, u32[]{:S(2)}) copy-start(bf16[1,128,512]{2,1,0:T(8,128)(2,1)} %param.5) | copy-start | bytes 393220
  3.4 0.8 copy-start.2
  4.2 0.8 copy-start.3

commit v2 on v1

v2 whole, which is shorter than its diff:
```python
import functools
import math

import jax
import jax.numpy as jnp
from jax import lax
from jax.experimental import pallas as pl
from jax.experimental.pallas import tpu as pltpu
from jax.sharding import PartitionSpec as P

HD = 128
PAD = 16
LAG = 1
MESH = pl.DeviceIdType.MESH
BF = jnp.bfloat16
F32 = jnp.float32


class Ring:
    def __init__(self, n, long_right, ref_of, blocks, send, recv, right, left):
        self.n = n
        self.reach = n // 2 if long_right else (n - 1) // 2
        self.ref_of, self.blocks, self.send, self.recv = ref_of, blocks, send, recv
        self.right, self.left = right, left

    def slots(self, s):
        return [s] * (s <= self.reach) + [self.n - s] * (s <= self.n - 1 - self.reach)

    def pass_to(self, j):
        rightward = j <= self.reach
        pltpu.make_async_remote_copy(
            src_ref=self.ref_of(j - 1 if rightward else (j + 1) % self.n, 0),
            dst_ref=self.ref_of(j, 1 if rightward else -1),
            send_sem=self.send,
            recv_sem=self.recv(j if rightward else self.n - j),
            device_id=self.right if rightward else self.left,
            device_id_type=MESH,
        ).start()

    def begin(self):
        for j in self.slots(1):
            self.pass_to(j)

    def forward(self, s):
        onward = self.slots(s + 1)
        for j in self.slots(s):
            if j <= self.reach and s + 1 in onward and s + 1 <= self.reach:
                self.pass_to(s + 1)
            elif j > self.reach and self.n - s - 1 in onward and self.n - s - 1 > self.reach:
                self.pass_to(self.n - s - 1)
        return self.slots(s)

    def step(self, s):
        settle(self.blocks(len(self.slots(s))), self.recv(s))
        return self.forward(s)


def settle(ref, sem):
    pltpu.make_async_copy(ref, ref, sem).wait()


def kernel(
    sizes, span_in, q, k, v, cot, att, grad,
    span, kbuf, vbuf, q4, scores, tops, probs, cbuf, cot_t, abuf, acc, out1, in1, out2, in2, last,
    sent, kv_recv, y_recv, a2a_recv, own_sem, x_recv, att_recv, in_sem, q_sem, att_sem, grad_sem,
):
    n_pipe, nz, nx = sizes
    p, c, t = lax.axis_index("pipe"), lax.axis_index("ctx"), lax.axis_index("tp")
    side = lax.rem(c, 2)
    z = lax.div(c, 2)
    tokens = q.shape[0]
    heads = q.shape[1] // HD
    span_len = tokens // 2
    feats = cot.shape[1] // nz
    chunk = tokens // nx
    half = feats // 2

    def at_z(d):
        return {"ctx": lax.rem(z + d, nz) * 2 + side}

    def at_x(d):
        return {"tp": lax.rem(t + d, nx)}

    across = c + 1 - 2 * side
    mirror = lax.rem(p + n_pipe // 2, n_pipe)
    y_peer = {"ctx": across}
    fold_peer = {"pipe": mirror, "ctx": across}
    pair_peer = {"pipe": mirror}

    barrier = pltpu.get_barrier_semaphore()
    peers = [at_z(d) for d in range(1, nz)] + [y_peer, fold_peer, pair_peer, at_x(1), at_x(nx - 1)]
    for peer in peers:
        pl.semaphore_signal(barrier, inc=1, device_id=peer, device_id_type=MESH)

    span_load = pltpu.make_async_copy(span_in, span, in_sem.at[0])
    k_load = pltpu.make_async_copy(k, kbuf.at[0, 0:tokens], in_sem.at[1])
    v_load = pltpu.make_async_copy(v, vbuf.at[0], in_sem.at[2])
    q_load = [
        pltpu.make_async_copy(
            q.at[:, h * HD:(h + 1) * HD], q4.at[h * tokens:(h + 1) * tokens, :], q_sem)
        for h in range(heads)
    ]
    for copy in [span_load, k_load, v_load] + q_load:
        copy.start()
    span_load.wait()
    lane = lax.broadcasted_iota(jnp.int32, (PAD, HD), 1)
    id0, id1 = span[0, 0].astype(F32), span[0, 1].astype(F32)
    kbuf[0, tokens:, :] = jnp.where(lane < span_len, id0, id1).astype(BF)
    k_load.wait()
    v_load.wait()
    pl.semaphore_wait(barrier, len(peers))

    def z_ring(buf, base, g, long_right):
        return Ring(
            nz, long_right, lambda j, way: buf.at[base + j], lambda count: buf.at[0:count],
            sent.at[g % 2], lambda s: kv_recv.at[g, s - 1], at_z(1), at_z(nz - 1),
        )

    k_own = z_ring(kbuf, 0, 0, True)
    v_own = z_ring(vbuf, 0, 1, False)
    k_far = z_ring(kbuf, nz, 2, False)
    v_far = z_ring(vbuf, nz, 3, True)
    k_over = pltpu.make_async_remote_copy(
        kbuf.at[0], kbuf.at[nz], sent.at[0], y_recv.at[0], device_id=y_peer, device_id_type=MESH)
    v_over = pltpu.make_async_remote_copy(
        vbuf.at[0], vbuf.at[nz], sent.at[1], y_recv.at[1], device_id=y_peer, device_id_type=MESH)
    k_own.begin()
    k_over.start()
    v_own.begin()
    v_over.start()

    rows = pl.ds(pl.multiple_of(t * chunk, chunk), chunk)

    def to_z(d):
        columns = pl.ds(pl.multiple_of(lax.rem(z + d, nz) * feats, feats), feats)
        return cot.at[rows, columns]

    own_cot = pltpu.make_async_copy(to_z(0), cbuf.at[t, 0], own_sem)
    own_cot.start()
    a2a = {
        d: pltpu.make_async_remote_copy(
            to_z(d), cbuf.at[t, d], sent.at[2], a2a_recv.at[d // (nz // 2)], device_id=at_z(d), device_id_type=MESH)
        for d in range(1, nz)
    }
    by_reach = {}
    for d in range(1, nz):
        by_reach.setdefault(min(d, nz - d), []).append(d)

    for reach in sorted(by_reach, reverse=True):
        for d in by_reach[reach]:
            a2a[d].start()

    row = lax.broadcasted_iota(jnp.int32, (tokens, HD), 0)
    col = lax.broadcasted_iota(jnp.int32, (tokens, HD), 1)
    query_pos = jnp.where(row < span_len, id0, id1) * span_len + lax.rem(row, span_len).astype(F32)
    key_off = lax.rem(col, span_len).astype(F32)

    settle(q4, q_sem)

    factor = math.log2(math.e) / math.sqrt(HD)

    def score(slot):
        keys = kbuf[slot, :tokens, :]
        ids = kbuf[slot, tokens:, :].astype(F32)
        key_pos = jnp.broadcast_to(ids[0:1, :], (tokens, HD)) * span_len + key_off
        bias = jnp.where(key_pos <= query_pos, 0.0, -1e30)
        for h in range(heads):
            part = lax.dot_general(
                q4[h * tokens:(h + 1) * tokens, :], keys, (((1,), (1,)), ((), ())), preferred_element_type=F32)
            part = part * factor + bias
            scores[h, slot] = part
            tops[h] = part if slot == 0 else jnp.maximum(tops[h], part)

    score(0)
    steps = nz // 2
    x_steps = nx // 2
    low, high = (0, nz // 2), (nz // 2, nz)

    def x_ring(part, long_right):
        def ref_of(j, way):
            place = lax.rem(t + way - j + 2 * nx, nx)
            return cbuf.at[place, part[0]:part[1]]

        return Ring(nx, long_right, ref_of, None, sent.at[3], lambda s: x_recv.at[s - 1], at_x(1), at_x(nx - 1))

    x_low, x_high = x_ring(low, True), x_ring(high, False)

    def x_step(s):
        if s <= x_steps:
            settle(cbuf.at[0:(len(x_low.slots(s)) + len(x_high.slots(s))) // 2], x_recv.at[s - 1])
            x_low.forward(s)
            x_high.forward(s)

    def own_step(s):
        fresh = k_own.step(s)
        v_own.step(s)
        return fresh

    def far_step(s):
        fresh = [nz + slot for slot in k_far.step(s)]
        v_far.step(s)
        return fresh

    def over():
        k_over.wait_recv()
        k_far.begin()
        v_over.wait_recv()
        v_far.begin()
        return [nz]

    def x_begin():
        own_cot.wait()
        settle(cbuf.at[t, 1:nz // 2], a2a_recv.at[0])
        x_low.begin()
        settle(cbuf.at[t, nz // 2:nz], a2a_recv.at[1])
        x_high.begin()

    lag = min(LAG, steps)
    for s in range(1, steps + lag + 1):
        fresh = []
        if s <= steps:
            fresh += own_step(s)
        if s == lag:
            fresh += over()
        if s > lag:
            fresh += far_step(s - lag)
        if s == 2:
            x_begin()
        if s == steps:
            x_step(1)
        for slot in fresh:
            score(slot)

    a_rings = [
        Ring(
            nz, h % 2 == 0, functools.partial(lambda h, j, way: abuf.at[h, j], h),
            functools.partial(lambda h, count: abuf.at[h, 0:count], h), sent.at[4],
            functools.partial(lambda h, s: att_recv.at[h, s - 1], h), at_z(1), at_z(nz - 1))
        for h in range(heads)
    ]

    def attend(h):
        top = jnp.broadcast_to(jnp.max(tops[h], axis=-1, keepdims=True), (tokens, HD))
        total = jnp.zeros((tokens, HD), F32)
        for slot in range(2 * nz):
            weights = jnp.exp2(scores[h, slot] - top)
            total = total + weights
            probs[:, slot * HD:(slot + 1) * HD] = weights.astype(BF)
        mixed = jnp.dot(probs[...], vbuf[...].reshape(2 * nz * tokens, HD), preferred_element_type=F32)
        out = (mixed / jnp.sum(total, axis=-1, keepdims=True)).astype(BF)
        abuf[h, 0] = out

    att_out = [
        pltpu.make_async_copy(abuf.at[h, 0], att.at[:, h * HD:(h + 1) * HD], att_sem) for h in range(heads)
    ]
    for h in range(heads):
        attend(h)
        a_rings[h].begin()
        if h == 1:
            x_step(2)
    for copy in att_out:
        copy.start()

    def turn(j):
        block = cbuf[:, j].reshape(tokens, feats)
        cot_t[:, j * tokens:(j + 1) * tokens] = block.T

    for s in range(1, steps):
        for h in range(heads):
            a_rings[h].step(s)
        if s == 1:
            x_step(3)
        if s == steps - 1:
            x_step(4)
    for j in range(nz):
        turn(j)

    fold = [
        pltpu.make_async_remote_copy(
            out1.at[h, 1 - side], in1.at[h], sent.at[5], y_recv.at[2 + h],
            device_id=fold_peer, device_id_type=MESH)
        for h in range(heads)
    ]
    pair = [
        pltpu.make_async_remote_copy(
            out2.at[h], in2.at[h], sent.at[6], y_recv.at[2 + heads + h],
            device_id=pair_peer, device_id_type=MESH)
        for h in range(heads)
    ]
    for h in range(heads):
        a_rings[h].step(steps)
        summed = jnp.dot(cot_t[...], abuf[h].reshape(nz * tokens, HD), preferred_element_type=F32)
        acc[h] = summed.reshape(2, half, HD)
        out1[h] = summed.astype(BF).reshape(2, half, HD)
        fold[h].start()
    for h in range(heads):
        fold[h].wait_recv()
        both = acc[h, side] + in1[h].astype(F32)
        acc[h, side] = both
        out2[h] = both.astype(BF)
        pair[h].start()
    grad_out = [
        pltpu.make_async_copy(last.at[h], grad.at[:, h * HD:(h + 1) * HD], grad_sem) for h in range(heads)
    ]
    for h in range(heads):
        pair[h].wait_recv()
        last[h] = (acc[h, side] + in2[h].astype(F32)).astype(BF)
        grad_out[h].start()

    for g, ref in enumerate(
        [kbuf.at[1:2 * nz], vbuf.at[1:2 * nz], cbuf.at[0, 1:nz], cbuf.at[0:nx - 1], abuf.at[:, 1:nz], in1, in2]
    ):
        settle(ref, sent.at[g])
    settle(att, att_sem)
    settle(grad, grad_sem)


def solution(mesh):
    n_pipe, n_ctx, nx = mesh.shape["pipe"], mesh.shape["ctx"], mesh.shape["tp"]
    nz = n_ctx // 2

    def local(queries, keys, values, span_ids, cotangent):
        tokens, width = queries.shape[1:]
        heads = width // HD
        feats = cotangent.shape[2] // nz
        half = feats // 2
        dma = pltpu.SemaphoreType.DMA
        hbm = pl.BlockSpec(memory_space=pltpu.HBM)
        attention, grad = pl.pallas_call(
            functools.partial(kernel, (n_pipe, nz, nx)),
            out_shape=(
                jax.ShapeDtypeStruct((tokens, width), BF),
                jax.ShapeDtypeStruct((half, width), BF),
            ),
            in_specs=[hbm] * 5,
            out_specs=(hbm, hbm),
            scratch_shapes=[
                pltpu.SMEM((1, 2), jnp.int32),
                pltpu.VMEM((2 * nz, tokens + PAD, HD), BF),
                pltpu.VMEM((2 * nz, tokens, HD), BF),
                pltpu.VMEM((heads * tokens, HD), BF),
                pltpu.VMEM((heads, 2 * nz, tokens, HD), F32),
                pltpu.VMEM((heads, tokens, HD), F32),
                pltpu.VMEM((tokens, 2 * nz * HD), BF),
                pltpu.VMEM((nx, nz, tokens // nx, feats), BF),
                pltpu.VMEM((feats, nz * tokens), BF),
                pltpu.VMEM((heads, nz, tokens, HD), BF),
                pltpu.VMEM((heads, 2, half, HD), F32),
                pltpu.VMEM((heads, 2, half, HD), BF),
                pltpu.VMEM((heads, half, HD), BF),
                pltpu.VMEM((heads, half, HD), BF),
                pltpu.VMEM((heads, half, HD), BF),
                pltpu.VMEM((heads, half, HD), BF),
                dma((7,)),
                dma((4, nz // 2)),
                dma((2 + 2 * heads,)),
                dma((2,)),
                dma,
                dma((nx // 2,)),
                dma((heads, nz // 2)),
                dma((3,)),
                dma,
                dma,
                dma,
            ],
            compiler_params=pltpu.CompilerParams(
                collective_id=0, has_side_effects=True, vmem_limit_bytes=41943040
            ),
            name="fused",
        )(*[pltpu.with_memory_space_constraint(a, pltpu.HBM) for a in (span_ids, queries[0], keys[0], values[0], cotangent[0])])
        return attention[None], grad[None]

    return jax.shard_map(
        local,
        mesh=mesh,
        in_specs=(
            P("pipe", "ctx", "tp"),
            P("pipe", "ctx", "tp"),
            P("pipe", "ctx", "tp"),
            P("pipe", "ctx"),
            P("pipe", "ctx", None),
        ),
        out_specs=(P("pipe", "ctx", "tp"), P("pipe", "ctx", "tp")),
        check_vma=False,
    )
```

time: 86.5 us -> 74.8 us (0.86)
  the two profiles are of different devices: /device:TPU:4 before, /device:TPU:6 now
where the time goes in v2:
time: 74.8 us; the launch traced here: 74.6 us
  Pallas kernels  72.6 us (97%)
  local copies, waits for them, and re-layouts  1.36 us (2%)
    pallas_call x1, Pallas kernels, local(): pl.pallas_call(functools.partial(kernel, (n_pipe, nz, nx)), out_shape=(ja...  72.6 us

profile of v2, /device:TPU:6, one launch (start us, length us, event | category | flops | bytes accessed | tf_op | source)
XLA Modules:
  0.0 74.6 jit_solution(8431514419398319256)
XLA Ops:
  0.6 72.6 %fused.1 = (bf16[128,512]{1,0:T(8,128)(2,1)S(1)}, bf16[256,512]{1,0:T(8,128)(2,1)S(1)}) custom-call(s32[1,2]{1,0:T(1,128)} %span_in.1, bf16[128,512]{1,0:T(8,128)(2,1)} %bitcast.9, bf16[128,128]{1,0:T(8,128)(2,1)} %bitcast.10, bf16[128,128]{1,0:T(8,128)(2,1)} %bitcast.11, bf16[128,4096]{1,0:T(8,128)(2,1)} %bitcast.8), custom_call_target="tpu_custom_call" | custom-call | tf_op jit(solution)/shard_map/fused/pallas_call | solution.py:329
  73.2 0.7 copy.9
  73.9 0.7 copy.10

commit v3 on v2

--- a/solution.py
+++ b/solution.py
@@ -10,49 +10,53 @@
 
 HD = 128
 PAD = 16
-LAG = 1
 MESH = pl.DeviceIdType.MESH
 BF = jnp.bfloat16
 F32 = jnp.float32
 
 
-class Ring:
-    def __init__(self, n, long_right, ref_of, blocks, send, recv, right, left):
+class Spread:
+    def __init__(self, n, long_right, ref_of, blocks, send, recv, at):
         self.n = n
         self.reach = n // 2 if long_right else (n - 1) // 2
-        self.ref_of, self.blocks, self.send, self.recv = ref_of, blocks, send, recv
-        self.right, self.left = right, left
-
-    def slots(self, s):
-        return [s] * (s <= self.reach) + [self.n - s] * (s <= self.n - 1 - self.reach)
-
-    def pass_to(self, j):
-        rightward = j <= self.reach
-        pltpu.make_async_remote_copy(
-            src_ref=self.ref_of(j - 1 if rightward else (j + 1) % self.n, 0),
-            dst_ref=self.ref_of(j, 1 if rightward else -1),
-            send_sem=self.send,
-            recv_sem=self.recv(j if rightward else self.n - j),
-            device_id=self.right if rightward else self.left,
-            device_id_type=MESH,
-        ).start()
+        self.ref_of, self.blocks, self.send, self.recv, self.at = ref_of, blocks, send, recv, at
+
+    def slots(self, group):
+        rightward = [j for j in range(1, self.reach + 1) if min(j, 3) == group]
+        leftward = [self.n - d for d in range(1, self.n - self.reach) if min(d, 3) == group]
+        return rightward + leftward
+
+    def emit(self, group):
+        for j in self.slots(group):
+            rightward = j <= self.reach
+            apart = j if rightward else self.n - j
+            via = 2 if apart > 2 else 0
+            hop = apart - via
+            signed = hop if rightward else -hop
+            source = via if rightward else (self.n - via) % self.n
+            pltpu.make_async_remote_copy(
+                src_ref=self.ref_of(source, 0),
+                dst_ref=self.ref_of(j, signed),
+                send_sem=self.send,
+                recv_sem=self.recv(group),
+                device_id=self.at(signed),
+                device_id_type=MESH,
+            ).start()
 
     def begin(self):
-        for j in self.slots(1):
-            self.pass_to(j)
-
-    def forward(self, s):
-        onward = self.slots(s + 1)
-        for j in self.slots(s):
-            if j <= self.reach and s + 1 in onward and s + 1 <= self.reach:
-                self.pass_to(s + 1)
-            elif j > self.reach and self.n - s - 1 in onward and self.n - s - 1 > self.reach:
-                self.pass_to(self.n - s - 1)
-        return self.slots(s)
-
-    def step(self, s):
-        settle(self.blocks(len(self.slots(s))), self.recv(s))
-        return self.forward(s)
+        self.emit(2)
+        self.emit(1)
+
+    def take(self, group):
+        count = len(self.slots(group))
+        if count:
+            settle(self.blocks(count), self.recv(group))
+        return self.slots(group)
+
+    def relay(self):
+        slots = self.take(2)
+        self.emit(3)
+        return slots
 
 
 def settle(ref, sem):
@@ -76,10 +80,10 @@
     half = feats // 2
 
     def at_z(d):
-        return {"ctx": lax.rem(z + d, nz) * 2 + side}
+        return {"ctx": lax.rem(z + d + nz, nz) * 2 + side}
 
     def at_x(d):
-        return {"tp": lax.rem(t + d, nx)}
+        return {"tp": lax.rem(t + d + nx, nx)}
 
     across = c + 1 - 2 * side
     mirror = lax.rem(p + n_pipe // 2, n_pipe)
@@ -88,7 +92,8 @@
     pair_peer = {"pipe": mirror}
 
     barrier = pltpu.get_barrier_semaphore()
-    peers = [at_z(d) for d in range(1, nz)] + [y_peer, fold_peer, pair_peer, at_x(1), at_x(nx - 1)]
+    peers = [at_z(d) for d in range(1, nz)] + [y_peer, fold_peer, pair_peer]
+    peers += [at_x(d) for d in sorted({hop % nx for hop in (-2, -1, 1, 2)} - {0})]
     for peer in peers:
         pl.semaphore_signal(barrier, inc=1, device_id=peer, device_id_type=MESH)
 
@@ -111,9 +116,9 @@
     pl.semaphore_wait(barrier, len(peers))
 
     def z_ring(buf, base, g, long_right):
-        return Ring(
+        return Spread(
             nz, long_right, lambda j, way: buf.at[base + j], lambda count: buf.at[0:count],
-            sent.at[g % 2], lambda s: kv_recv.at[g, s - 1], at_z(1), at_z(nz - 1),
+            sent.at[g % 2], lambda group: kv_recv.at[g, group - 1], at_z,
         )
 
     k_own = z_ring(kbuf, 0, 0, True)
@@ -172,8 +177,6 @@
             tops[h] = part if slot == 0 else jnp.maximum(tops[h], part)
 
     score(0)
-    steps = nz // 2
-    x_steps = nx // 2
     low, high = (0, nz // 2), (nz // 2, nz)
 
     def x_ring(part, long_right):
@@ -181,61 +184,49 @@
             place = lax.rem(t + way - j + 2 * nx, nx)
             return cbuf.at[place, part[0]:part[1]]
 
-        return Ring(nx, long_right, ref_of, None, sent.at[3], lambda s: x_recv.at[s - 1], at_x(1), at_x(nx - 1))
+        return Spread(nx, long_right, ref_of, None, sent.at[3], lambda group: x_recv.at[group - 1], at_x)
 
     x_low, x_high = x_ring(low, True), x_ring(high, False)
 
-    def x_step(s):
-        if s <= x_steps:
-            settle(cbuf.at[0:(len(x_low.slots(s)) + len(x_high.slots(s))) // 2], x_recv.at[s - 1])
-            x_low.forward(s)
-            x_high.forward(s)
-
-    def own_step(s):
-        fresh = k_own.step(s)
-        v_own.step(s)
-        return fresh
-
-    def far_step(s):
-        fresh = [nz + slot for slot in k_far.step(s)]
-        v_far.step(s)
-        return fresh
-
-    def over():
-        k_over.wait_recv()
-        k_far.begin()
-        v_over.wait_recv()
-        v_far.begin()
-        return [nz]
-
-    def x_begin():
-        own_cot.wait()
-        settle(cbuf.at[t, 1:nz // 2], a2a_recv.at[0])
-        x_low.begin()
-        settle(cbuf.at[t, nz // 2:nz], a2a_recv.at[1])
-        x_high.begin()
-
-    lag = min(LAG, steps)
-    for s in range(1, steps + lag + 1):
-        fresh = []
-        if s <= steps:
-            fresh += own_step(s)
-        if s == lag:
-            fresh += over()
-        if s > lag:
-            fresh += far_step(s - lag)
-        if s == 2:
-            x_begin()
-        if s == steps:
-            x_step(1)
-        for slot in fresh:
-            score(slot)
+    def x_take(group):
+        count = len(x_low.slots(group)) + len(x_high.slots(group))
+        if count:
+            settle(cbuf.at[0:count // 2], x_recv.at[group - 1])
+
+    fresh = k_own.relay()
+    v_own.relay()
+    k_over.wait_recv()
+    k_far.begin()
+    v_over.wait_recv()
+    v_far.begin()
+    for slot in fresh + k_own.take(1) + [nz]:
+        score(slot)
+    own_cot.wait()
+    settle(cbuf.at[t, 1:nz // 2], a2a_recv.at[0])
+    x_low.begin()
+    settle(cbuf.at[t, nz // 2:nz], a2a_recv.at[1])
+    x_high.begin()
+    for slot in k_own.take(3):
+        score(slot)
+    fresh = k_far.relay()
+    v_far.relay()
+    for slot in fresh + k_far.take(1):
+        score(nz + slot)
+    x_take(2)
+    x_low.emit(3)
+    x_high.emit(3)
+    for slot in k_far.take(3):
+        score(nz + slot)
+    v_own.take(1)
+    v_own.take(3)
+    v_far.take(1)
+    v_far.take(3)
 
     a_rings = [
-        Ring(
+        Spread(
             nz, h % 2 == 0, functools.partial(lambda h, j, way: abuf.at[h, j], h),
             functools.partial(lambda h, count: abuf.at[h, 0:count], h), sent.at[4],
-            functools.partial(lambda h, s: att_recv.at[h, s - 1], h), at_z(1), at_z(nz - 1))
+            functools.partial(lambda h, group: att_recv.at[h, group - 1], h), at_z)
         for h in range(heads)
     ]
 
@@ -256,8 +247,6 @@
     for h in range(heads):
         attend(h)
         a_rings[h].begin()
-        if h == 1:
-            x_step(2)
     for copy in att_out:
         copy.start()
 
@@ -265,15 +254,14 @@
         block = cbuf[:, j].reshape(tokens, feats)
         cot_t[:, j * tokens:(j + 1) * tokens] = block.T
 
-    for s in range(1, steps):
-        for h in range(heads):
-            a_rings[h].step(s)
-        if s == 1:
-            x_step(3)
-        if s == steps - 1:
-            x_step(4)
+    x_take(1)
+    x_take(3)
     for j in range(nz):
         turn(j)
+    for h in range(heads):
+        a_rings[h].relay()
+    for h in range(heads):
+        a_rings[h].take(1)
 
     fold = [
         pltpu.make_async_remote_copy(
@@ -288,7 +276,7 @@
         for h in range(heads)
     ]
     for h in range(heads):
-        a_rings[h].step(steps)
+        a_rings[h].take(3)
         summed = jnp.dot(cot_t[...], abuf[h].reshape(nz * tokens, HD), preferred_element_type=F32)
         acc[h] = summed.reshape(2, half, HD)
         out1[h] = summed.astype(BF).reshape(2, half, HD)
@@ -352,12 +340,12 @@
                 pltpu.VMEM((heads, half, HD), BF),
                 pltpu.VMEM((heads, half, HD), BF),
                 dma((7,)),
-                dma((4, nz // 2)),
+                dma((4, 3)),
                 dma((2 + 2 * heads,)),
                 dma((2,)),
                 dma,
-                dma((nx // 2,)),
-                dma((heads, nz // 2)),
+                dma((3,)),
+                dma((heads, 3)),
                 dma((3,)),
                 dma,
                 dma,

time: 74.8 us -> 74.3 us (level)
  the two profiles are of different devices: /device:TPU:6 before, /device:TPU:4 now
where the time goes in v3:
time: 74.3 us; the launch traced here: 74.1 us
  Pallas kernels  72.1 us (97%)
  local copies, waits for them, and re-layouts  1.36 us (2%)
    pallas_call x1, Pallas kernels, local(): pl.pallas_call(functools.partial(kernel, (n_pipe, nz, nx)), out_shape=(ja...  72.1 us

profile of v3, /device:TPU:4, one launch (start us, length us, event | category | flops | bytes accessed | tf_op | source)
XLA Modules:
  0.0 74.1 jit_solution(9446661136181978693)
XLA Ops:
  0.6 72.1 %fused.1 = (bf16[128,512]{1,0:T(8,128)(2,1)S(1)}, bf16[256,512]{1,0:T(8,128)(2,1)S(1)}) custom-call(s32[1,2]{1,0:T(1,128)} %span_in.1, bf16[128,512]{1,0:T(8,128)(2,1)} %bitcast.9, bf16[128,128]{1,0:T(8,128)(2,1)} %bitcast.10, bf16[128,128]{1,0:T(8,128)(2,1)} %bitcast.11, bf16[128,4096]{1,0:T(8,128)(2,1)} %bitcast.8), custom_call_target="tpu_custom_call" | custom-call | tf_op jit(solution)/shard_map/fused/pallas_call | solution.py:317
  72.7 0.7 copy.9
  73.4 0.7 copy.10

commit v4 on v3

--- a/solution.py
+++ b/solution.py
@@ -16,7 +16,8 @@
 
 
 class Spread:
-    def __init__(self, n, long_right, ref_of, blocks, send, recv, at):
+    def __init__(self, n, long_right, ref_of, blocks, send, recv, at, straight=False):
+        self.straight = straight
         self.n = n
         self.reach = n // 2 if long_right else (n - 1) // 2
         self.ref_of, self.blocks, self.send, self.recv, self.at = ref_of, blocks, send, recv, at
@@ -30,7 +31,7 @@
         for j in self.slots(group):
             rightward = j <= self.reach
             apart = j if rightward else self.n - j
-            via = 2 if apart > 2 else 0
+            via = 2 if apart > 2 else 0 if self.straight else apart - 1
             hop = apart - via
             signed = hop if rightward else -hop
             source = via if rightward else (self.n - via) % self.n
@@ -44,7 +45,8 @@
             ).start()
 
     def begin(self):
-        self.emit(2)
+        if self.straight:
+            self.emit(2)
         self.emit(1)
 
     def take(self, group):
@@ -53,9 +55,9 @@
             settle(self.blocks(count), self.recv(group))
         return self.slots(group)
 
-    def relay(self):
-        slots = self.take(2)
-        self.emit(3)
+    def relay(self, group):
+        slots = self.take(group)
+        self.emit(group + 1)
         return slots
 
 
@@ -154,7 +156,6 @@
     for reach in sorted(by_reach, reverse=True):
         for d in by_reach[reach]:
             a2a[d].start()
-
     row = lax.broadcasted_iota(jnp.int32, (tokens, HD), 0)
     col = lax.broadcasted_iota(jnp.int32, (tokens, HD), 1)
     query_pos = jnp.where(row < span_len, id0, id1) * span_len + lax.rem(row, span_len).astype(F32)
@@ -184,7 +185,7 @@
             place = lax.rem(t + way - j + 2 * nx, nx)
             return cbuf.at[place, part[0]:part[1]]
 
-        return Spread(nx, long_right, ref_of, None, sent.at[3], lambda group: x_recv.at[group - 1], at_x)
+        return Spread(nx, long_right, ref_of, None, sent.at[3], lambda group: x_recv.at[group - 1], at_x, True)
 
     x_low, x_high = x_ring(low, True), x_ring(high, False)
 
@@ -193,33 +194,36 @@
         if count:
             settle(cbuf.at[0:count // 2], x_recv.at[group - 1])
 
-    fresh = k_own.relay()
-    v_own.relay()
+    fresh = k_own.relay(1)
+    v_own.relay(1)
     k_over.wait_recv()
     k_far.begin()
     v_over.wait_recv()
     v_far.begin()
-    for slot in fresh + k_own.take(1) + [nz]:
+    for slot in fresh + [nz]:
         score(slot)
+    fresh = k_own.relay(2)
+    v_own.relay(2)
+    for slot in fresh:
+        score(slot)
+    fresh = k_far.relay(1)
+    v_far.relay(1)
+    for slot in fresh:
+        score(nz + slot)
     own_cot.wait()
     settle(cbuf.at[t, 1:nz // 2], a2a_recv.at[0])
     x_low.begin()
     settle(cbuf.at[t, nz // 2:nz], a2a_recv.at[1])
     x_high.begin()
+    fresh = k_far.relay(2)
+    v_far.relay(2)
+    for slot in fresh:
+        score(nz + slot)
     for slot in k_own.take(3):
         score(slot)
-    fresh = k_far.relay()
-    v_far.relay()
-    for slot in fresh + k_far.take(1):
-        score(nz + slot)
-    x_take(2)
-    x_low.emit(3)
-    x_high.emit(3)
     for slot in k_far.take(3):
         score(nz + slot)
-    v_own.take(1)
     v_own.take(3)
-    v_far.take(1)
     v_far.take(3)
 
     a_rings = [
@@ -247,6 +251,9 @@
     for h in range(heads):
         attend(h)
         a_rings[h].begin()
+    x_take(2)
+    x_low.emit(3)
+    x_high.emit(3)
     for copy in att_out:
         copy.start()
 
@@ -254,14 +261,14 @@
         block = cbuf[:, j].reshape(tokens, feats)
         cot_t[:, j * tokens:(j + 1) * tokens] = block.T
 
+    for h in range(heads):
+        a_rings[h].relay(1)
+    for h in range(heads):
+        a_rings[h].relay(2)
     x_take(1)
     x_take(3)
     for j in range(nz):
         turn(j)
-    for h in range(heads):
-        a_rings[h].relay()
-    for h in range(heads):
-        a_rings[h].take(1)
 
     fold = [
         pltpu.make_async_remote_copy(

time: 74.3 us -> 70.8 us (0.953)
  Pallas kernels: 72.1 us -> 68.6 us
    pallas_call x1, Pallas kernels: 72.1 us -> 68.6 us  [local(): pl.pallas_call(functools.partial(kernel, (n_pipe, nz, nx)), out_shape=(ja...]
where the time goes in v4:
time: 70.8 us; the launch traced here: 70.6 us
  Pallas kernels  68.6 us (97%)
  local copies, waits for them, and re-layouts  1.36 us (2%)
    pallas_call x1, Pallas kernels, local(): pl.pallas_call(functools.partial(kernel, (n_pipe, nz, nx)), out_shape=(ja...  68.6 us

profile of v4, /device:TPU:4, one launch (start us, length us, event | category | flops | bytes accessed | tf_op | source)
XLA Modules:
  0.0 70.6 jit_solution(14856307828788889365)
XLA Ops:
  0.6 68.6 %fused.1 = (bf16[128,512]{1,0:T(8,128)(2,1)S(1)}, bf16[256,512]{1,0:T(8,128)(2,1)S(1)}) custom-call(s32[1,2]{1,0:T(1,128)} %span_in.1, bf16[128,512]{1,0:T(8,128)(2,1)} %bitcast.9, bf16[128,128]{1,0:T(8,128)(2,1)} %bitcast.10, bf16[128,128]{1,0:T(8,128)(2,1)} %bitcast.11, bf16[128,4096]{1,0:T(8,128)(2,1)} %bitcast.8), custom_call_target="tpu_custom_call" | custom-call | tf_op jit(solution)/shard_map/fused/pallas_call | solution.py:324
  69.2 0.7 copy.9
  69.9 0.7 copy.10

commit v5 on v4

--- a/solution.py
+++ b/solution.py
@@ -68,7 +68,7 @@
 def kernel(
     sizes, span_in, q, k, v, cot, att, grad,
     span, kbuf, vbuf, q4, scores, tops, probs, cbuf, cot_t, abuf, acc, out1, in1, out2, in2, last,
-    sent, kv_recv, y_recv, a2a_recv, own_sem, x_recv, att_recv, in_sem, q_sem, att_sem, grad_sem,
+    sent, kv_recv, y_recv, a2a_recv, own_sem, x_recv, att_recv, in_sem, q_sem, att_sem, grad_sem, known,
 ):
     n_pipe, nz, nx = sizes
     p, c, t = lax.axis_index("pipe"), lax.axis_index("ctx"), lax.axis_index("tp")
@@ -94,7 +94,8 @@
     pair_peer = {"pipe": mirror}
 
     barrier = pltpu.get_barrier_semaphore()
-    peers = [at_z(d) for d in range(1, nz)] + [y_peer, fold_peer, pair_peer]
+    beside = [at_z(d) for d in sorted({1, nz - 1})]
+    peers = beside + [fold_peer, pair_peer]
     peers += [at_x(d) for d in sorted({hop % nx for hop in (-2, -1, 1, 2)} - {0})]
     for peer in peers:
         pl.semaphore_signal(barrier, inc=1, device_id=peer, device_id_type=MESH)
@@ -117,6 +118,15 @@
     v_load.wait()
     pl.semaphore_wait(barrier, len(peers))
 
+    def tell(step, targets):
+        for target in targets:
+            pl.semaphore_signal(known.at[step], inc=1, device_id=target, device_id_type=MESH)
+
+    tell(0, [pair_peer])
+    rounds = min(nz // 2 - 1, 3)
+    if rounds:
+        tell(1, beside)
+
     def z_ring(buf, base, g, long_right):
         return Spread(
             nz, long_right, lambda j, way: buf.at[base + j], lambda count: buf.at[0:count],
@@ -132,8 +142,9 @@
     v_over = pltpu.make_async_remote_copy(
         vbuf.at[0], vbuf.at[nz], sent.at[1], y_recv.at[1], device_id=y_peer, device_id_type=MESH)
     k_own.begin()
+    v_own.begin()
+    pl.semaphore_wait(known.at[0], 1)
     k_over.start()
-    v_own.begin()
     v_over.start()
 
     rows = pl.ds(pl.multiple_of(t * chunk, chunk), chunk)
@@ -153,9 +164,17 @@
     for d in range(1, nz):
         by_reach.setdefault(min(d, nz - d), []).append(d)
 
-    for reach in sorted(by_reach, reverse=True):
-        for d in by_reach[reach]:
-            a2a[d].start()
+    for d in by_reach[1]:
+        a2a[d].start()
+
+    def learn(step):
+        if step <= rounds:
+            pl.semaphore_wait(known.at[step], len(beside))
+            if step < rounds:
+                tell(step + 1, beside)
+            for d in by_reach[step + 1]:
+                a2a[d].start()
+
     row = lax.broadcasted_iota(jnp.int32, (tokens, HD), 0)
     col = lax.broadcasted_iota(jnp.int32, (tokens, HD), 1)
     query_pos = jnp.where(row < span_len, id0, id1) * span_len + lax.rem(row, span_len).astype(F32)
@@ -194,12 +213,15 @@
         if count:
             settle(cbuf.at[0:count // 2], x_recv.at[group - 1])
 
+    learn(1)
     fresh = k_own.relay(1)
     v_own.relay(1)
+    learn(2)
     k_over.wait_recv()
     k_far.begin()
     v_over.wait_recv()
     v_far.begin()
+    learn(3)
     for slot in fresh + [nz]:
         score(slot)
     fresh = k_own.relay(2)
@@ -210,21 +232,19 @@
     v_far.relay(1)
     for slot in fresh:
         score(nz + slot)
+    fresh = k_far.relay(2)
+    v_far.relay(2)
     own_cot.wait()
     settle(cbuf.at[t, 1:nz // 2], a2a_recv.at[0])
     x_low.begin()
     settle(cbuf.at[t, nz // 2:nz], a2a_recv.at[1])
     x_high.begin()
-    fresh = k_far.relay(2)
-    v_far.relay(2)
     for slot in fresh:
         score(nz + slot)
     for slot in k_own.take(3):
         score(slot)
     for slot in k_far.take(3):
         score(nz + slot)
-    v_own.take(3)
-    v_far.take(3)
 
     a_rings = [
         Spread(
@@ -241,6 +261,9 @@
             weights = jnp.exp2(scores[h, slot] - top)
             total = total + weights
             probs[:, slot * HD:(slot + 1) * HD] = weights.astype(BF)
+        if h == 0:
+            v_own.take(3)
+            v_far.take(3)
         mixed = jnp.dot(probs[...], vbuf[...].reshape(2 * nz * tokens, HD), preferred_element_type=F32)
         out = (mixed / jnp.sum(total, axis=-1, keepdims=True)).astype(BF)
         abuf[h, 0] = out
@@ -251,18 +274,18 @@
     for h in range(heads):
         attend(h)
         a_rings[h].begin()
+    for copy in att_out:
+        copy.start()
+
+    def turn(j):
+        block = cbuf[:, j].reshape(tokens, feats)
+        cot_t[:, j * tokens:(j + 1) * tokens] = block.T
+
+    for h in range(heads):
+        a_rings[h].relay(1)
     x_take(2)
     x_low.emit(3)
     x_high.emit(3)
-    for copy in att_out:
-        copy.start()
-
-    def turn(j):
-        block = cbuf[:, j].reshape(tokens, feats)
-        cot_t[:, j * tokens:(j + 1) * tokens] = block.T
-
-    for h in range(heads):
-        a_rings[h].relay(1)
     for h in range(heads):
         a_rings[h].relay(2)
     x_take(1)
@@ -357,6 +380,7 @@
                 dma,
                 dma,
                 dma,
+                pltpu.SemaphoreType.REGULAR((nz // 2,)),
             ],
             compiler_params=pltpu.CompilerParams(
                 collective_id=0, has_side_effects=True, vmem_limit_bytes=41943040

time: 70.8 us -> 71.9 us (1.016)
  Pallas kernels: 68.6 us -> 69.6 us
    pallas_call x1, Pallas kernels: 68.6 us -> 69.6 us  [local(): pl.pallas_call(functools.partial(kernel, (n_pipe, nz, nx)), out_shape=(ja...]
where the time goes in v5:
time: 71.9 us; the launch traced here: 71.6 us
  Pallas kernels  69.6 us (97%)
  local copies, waits for them, and re-layouts  1.36 us (2%)
    pallas_call x1, Pallas kernels, local(): pl.pallas_call(functools.partial(kernel, (n_pipe, nz, nx)), out_shape=(ja...  69.6 us

profile of v5, /device:TPU:4, one launch (start us, length us, event | category | flops | bytes accessed | tf_op | source)
XLA Modules:
  0.0 71.6 jit_solution(6633754131039488052)
XLA Ops:
  0.6 69.6 %fused.1 = (bf16[128,512]{1,0:T(8,128)(2,1)S(1)}, bf16[256,512]{1,0:T(8,128)(2,1)S(1)}) custom-call(s32[1,2]{1,0:T(1,128)} %span_in.1, bf16[128,512]{1,0:T(8,128)(2,1)} %bitcast.9, bf16[128,128]{1,0:T(8,128)(2,1)} %bitcast.10, bf16[128,128]{1,0:T(8,128)(2,1)} %bitcast.11, bf16[128,4096]{1,0:T(8,128)(2,1)} %bitcast.8), custom_call_target="tpu_custom_call" | custom-call | tf_op jit(solution)/shard_map/fused/pallas_call | solution.py:347
  70.3 0.7 copy.9
  70.9 0.7 copy.10

commit v6 on v5

--- a/solution.py
+++ b/solution.py
@@ -232,13 +232,13 @@
     v_far.relay(1)
     for slot in fresh:
         score(nz + slot)
-    fresh = k_far.relay(2)
-    v_far.relay(2)
     own_cot.wait()
     settle(cbuf.at[t, 1:nz // 2], a2a_recv.at[0])
     x_low.begin()
+    fresh = k_far.relay(2)
     settle(cbuf.at[t, nz // 2:nz], a2a_recv.at[1])
     x_high.begin()
+    v_far.relay(2)
     for slot in fresh:
         score(nz + slot)
     for slot in k_own.take(3):
@@ -274,6 +274,9 @@
     for h in range(heads):
         attend(h)
         a_rings[h].begin()
+    x_take(2)
+    x_low.emit(3)
+    x_high.emit(3)
     for copy in att_out:
         copy.start()
 
@@ -283,9 +286,6 @@
 
     for h in range(heads):
         a_rings[h].relay(1)
-    x_take(2)
-    x_low.emit(3)
-    x_high.emit(3)
     for h in range(heads):
         a_rings[h].relay(2)
     x_take(1)

time: 71.9 us -> 69.8 us (0.971)
  the two profiles are of different devices: /device:TPU:4 before, /device:TPU:20 now
where the time goes in v6:
time: 69.8 us; the launch traced here: 69.5 us
  Pallas kernels  67.5 us (97%)
  local copies, waits for them, and re-layouts  1.36 us (2%)
    pallas_call x1, Pallas kernels, local(): pl.pallas_call(functools.partial(kernel, (n_pipe, nz, nx)), out_shape=(ja...  67.5 us

profile of v6, /device:TPU:20, one launch (start us, length us, event | category | flops | bytes accessed | tf_op | source)
XLA Modules:
  0.0 69.5 jit_solution(11298486744473542766)
XLA Ops:
  0.6 67.5 %fused.1 = (bf16[128,512]{1,0:T(8,128)(2,1)S(1)}, bf16[256,512]{1,0:T(8,128)(2,1)S(1)}) custom-call(s32[1,2]{1,0:T(1,128)} %span_in.1, bf16[128,512]{1,0:T(8,128)(2,1)} %bitcast.9, bf16[128,128]{1,0:T(8,128)(2,1)} %bitcast.10, bf16[128,128]{1,0:T(8,128)(2,1)} %bitcast.11, bf16[128,4096]{1,0:T(8,128)(2,1)} %bitcast.8), custom_call_target="tpu_custom_call" | custom-call | tf_op jit(solution)/shard_map/fused/pallas_call | solution.py:347
  68.2 0.7 copy.9
  68.8 0.7 %copy.10 = bf16[1,256,512]{2,1,0:T(8,128)(2,1)} copy(bf16[1,256,512]{2,1,0:T(8,128)(2,1)S(1)} %bitcast.6) | data formatting | bytes 524288

commit v7 on v6

--- a/solution.py
+++ b/solution.py
@@ -305,12 +305,17 @@
             device_id=pair_peer, device_id_type=MESH)
         for h in range(heads)
     ]
+
+    def product(h, part):
+        features = cot_t[pl.ds(pl.multiple_of(part * half, half), half), :]
+        return jnp.dot(features, abuf[h].reshape(nz * tokens, HD), preferred_element_type=F32)
+
     for h in range(heads):
         a_rings[h].take(3)
-        summed = jnp.dot(cot_t[...], abuf[h].reshape(nz * tokens, HD), preferred_element_type=F32)
-        acc[h] = summed.reshape(2, half, HD)
-        out1[h] = summed.astype(BF).reshape(2, half, HD)
+        out1[h, 1 - side] = product(h, 1 - side).astype(BF)
         fold[h].start()
+    for h in range(heads):
+        acc[h, side] = product(h, side)
     for h in range(heads):
         fold[h].wait_recv()
         both = acc[h, side] + in1[h].astype(F32)

time: 69.8 us -> 69.4 us (level)
  the two profiles are of different devices: /device:TPU:20 before, /device:TPU:4 now
where the time goes in v7:
time: 69.4 us; the launch traced here: 69.2 us
  Pallas kernels  67.2 us (97%)
  local copies, waits for them, and re-layouts  1.36 us (2%)
    pallas_call x1, Pallas kernels, local(): pl.pallas_call(functools.partial(kernel, (n_pipe, nz, nx)), out_shape=(ja...  67.2 us

profile of v7, /device:TPU:4, one launch (start us, length us, event | category | flops | bytes accessed | tf_op | source)
XLA Modules:
  0.0 69.2 jit_solution(3914968282439456054)
XLA Ops:
  0.6 67.2 %fused.1 = (bf16[128,512]{1,0:T(8,128)(2,1)S(1)}, bf16[256,512]{1,0:T(8,128)(2,1)S(1)}) custom-call(s32[1,2]{1,0:T(1,128)} %span_in.1, bf16[128,512]{1,0:T(8,128)(2,1)} %bitcast.9, bf16[128,128]{1,0:T(8,128)(2,1)} %bitcast.10, bf16[128,128]{1,0:T(8,128)(2,1)} %bitcast.11, bf16[128,4096]{1,0:T(8,128)(2,1)} %bitcast.8), custom_call_target="tpu_custom_call" | custom-call | tf_op jit(solution)/shard_map/fused/pallas_call | solution.py:352
  67.8 0.7 copy.9
  68.5 0.7 %copy.10 = bf16[1,256,512]{2,1,0:T(8,128)(2,1)} copy(bf16[1,256,512]{2,1,0:T(8,128)(2,1)S(1)} %bitcast.6) | data formatting | bytes 524288
